TPU v7x, 32 devices: a whole 2x2x4 slice. The times are simulated.
32 devices in a mesh: wide: 16 (over z, y, x), narrow: 2 (over core).
Axes of the slice: x: 2, y: 2, z: 4, core: 2. Of those that a mesh axis runs over, the one named last changes fastest.
Arguments:
- t_amps: bfloat16 [512, 32768], P('wide', 'narrow'), may hold values from -6 to 6
- v_blocks: bfloat16 [2, 16, 64, 128, 128], P('narrow', 'wide'), may hold values from -0.25 to 0.25
- block_pos: int32 [2, 16, 64], P('narrow', 'wide'), may hold values from 0 to 2047, as said below
- block_count: int32 [2, 16], P('narrow', 'wide'), may hold values from 24 to 64, as said below
Outputs:
- ladder: float32 [512, 32768], P('narrow', 'wide')
Inputs may be any that keep to these rules, and one draw needn't show every extreme that they name: `block_pos`: within one tile the places of all 64 slots are distinct, and they lie in at most 64 distinct block rows. `block_count`: some tile holds exactly 64 stored blocks; loads are skewed, most tiles holding far fewer.
All inputs are finite; a program needn't handle non-finite values.
Results may differ from a plain program's by a relative error of at most 0.0003.
Values may be sent and summed in bfloat16 or wider, within the bound.
A program may use at most 320 MiB of HBM per device.

v0:
```python
import functools

import jax
import jax.numpy as jnp
from jax import lax
from jax.experimental import pallas as pl
from jax.experimental.pallas import tpu as pltpu
from jax.sharding import PartitionSpec as P

MESH = pl.DeviceIdType.MESH
PIECES = 2


def dense_shards(width, t_amps, v_blocks, block_pos, block_count):
    stored = v_blocks[0, 0]
    places = block_pos[0, 0]
    slot_count = block_count[0, 0]
    block_size = stored.shape[1]
    slot_total = stored.shape[0]
    row_blocks = t_amps.shape[1] // block_size
    col_blocks = width // (lax.axis_size("wide") * block_size)
    live_mask = (jnp.arange(slot_total, dtype=jnp.int32) < slot_count).astype(jnp.bfloat16)
    masked = stored * live_mask[:, None, None]
    dense_tile = jnp.zeros((row_blocks * col_blocks, block_size, block_size), jnp.bfloat16)
    dense_tile = dense_tile.at[places].add(masked)
    dense_tile = dense_tile.reshape(row_blocks, col_blocks, block_size, block_size)
    dense_tile = jnp.transpose(dense_tile, (0, 2, 1, 3)).reshape(row_blocks * block_size, col_blocks * block_size)
    gathered = lax.all_gather(t_amps, "wide", axis=0, tiled=True)
    partial_sum = jnp.dot(gathered, dense_tile, preferred_element_type=jnp.float32)
    return lax.psum_scatter(partial_sum, "narrow", scatter_dimension=0, tiled=True)


def ladder_kernel(depth, t, v_tile, meta_v, out, *scratch):
    held = scratch[: (2 * depth - 1) * PIECES]
    bufs = [held[b * PIECES:(b + 1) * PIECES] for b in range(2 * depth - 1)]
    (v_own, v_other, meta_in, meta, meta_other, runs, part, core_in, y_out, own_out, own_sem, lay_sem, bx_send, bx_recv, local_sem, az_send, az_recv, bz_send, bz_recv,
     ax_send, ax_recv, one_send, one_recv, core_send, core_recv, y_send, y_recv) = scratch[(2 * depth - 1) * PIECES:]
    wide, core = lax.axis_index("wide"), lax.axis_index("narrow")
    z, y, x = wide // 4, (wide // 2) % 2, wide % 2
    up, down = (wide + 4, core), (wide - 4, core)
    across = (wide + 1 - 2 * x, core)
    beside = (wide + 2 - 4 * y, core)
    twin = (wide, 1 - core)
    half = depth // 2
    pieces, row_blocks, chunk, unused = t.shape
    rows = pieces * chunk
    v = v_tile.at[0, 0]
    slots, size = v.shape[0], v.shape[1]
    col_blocks = out.shape[-1] // size
    second = row_blocks * 5 // 32
    first = row_blocks - second
    first_cols = pl.ds(0, first)
    second_cols = pl.ds(first, second)
    has_up, has_down = z < depth - 1, z > 0

    def copy(src, dst, send, recv, device):
        return pltpu.make_async_remote_copy(
            src_ref=src, dst_ref=dst, send_sem=send, recv_sem=recv, device_id=device, device_id_type=MESH
        )

    def place(b):
        if b == 0:
            return z, None
        if b < depth:
            return z - b, z >= b
        return z + (b - depth + 1), z + (b - depth + 1) < depth

    def guarded(cond, fn):
        if cond is None:
            fn()
        else:
            pl.when(cond)(fn)

    def both(a, b):
        return b if a is None else a if b is None else jnp.logical_and(a, b)

    def hops(b):
        moves = []
        if b < depth - 1:
            moves.append((b + 1, up, has_up, b))
        if b == 0 or depth <= b < 2 * depth - 2:
            landing = depth if b == 0 else b + 1
            moves.append((landing, down, has_down, depth - 1 + (landing - depth)))
        return moves

    def az(b, move, q):
        landing, device, unused, sem = move
        src = t.at[q, first_cols] if b == 0 else bufs[b][q].at[x, first_cols]
        return copy(src, bufs[landing][q].at[x, first_cols], az_send.at[sem, q], az_recv.at[landing, q], device)

    def bz(b, move, q):
        landing, device, unused, sem = move
        return copy(bufs[b][q].at[:, second_cols], bufs[landing][q].at[:, second_cols], bz_send.at[sem, q], bz_recv.at[landing, q], device)

    def ax(b, q):
        src = t.at[q, first_cols] if b == 0 else bufs[b][q].at[x, first_cols]
        return copy(src, bufs[b][q].at[x, first_cols], ax_send.at[b, q], ax_recv.at[b, q], across)

    def az_wait(b, q):
        dst = bufs[b][q].at[x, first_cols]
        copy(dst, dst, az_send.at[0, q], az_recv.at[b, q], up).wait_recv()

    def bz_wait(b):
        for q in range(PIECES):
            dst = bufs[b][q].at[:, second_cols]
            copy(dst, dst, bz_send.at[0, q], bz_recv.at[b, q], up).wait_recv()

    def ax_wait(b, qs):
        for q in qs:
            dst = bufs[b][q].at[1 - x, first_cols]
            copy(dst, dst, ax_send.at[b, q], ax_recv.at[b, q], across).wait_recv()

    own_v = pltpu.make_async_copy(v, v_own, local_sem.at[1])
    own_m = pltpu.make_async_copy(meta_v, meta, local_sem.at[3])

    lays = [pltpu.make_async_copy(t.at[q], bufs[0][q].at[x], lay_sem.at[q]) for q in range(PIECES)]
    for lay in lays:
        lay.start()
    own_v.start()
    own_m.start()
    barrier = pltpu.get_barrier_semaphore()
    for device in (across, beside, twin):
        pl.semaphore_signal(barrier, inc=1, device_id=device, device_id_type=MESH)
    pl.when(has_up)(lambda: pl.semaphore_signal(barrier, inc=1, device_id=up, device_id_type=MESH))
    pl.when(has_down)(lambda: pl.semaphore_signal(barrier, inc=1, device_id=down, device_id_type=MESH))
    pl.semaphore_wait(barrier, 3 + has_up.astype(jnp.int32) + has_down.astype(jnp.int32))

    bxs = [copy(t.at[q, second_cols], bufs[0][q].at[x, second_cols], bx_send.at[q], bx_recv.at[q], across)
           for q in range(PIECES)]
    vy = copy(v, v_other, one_send.at[1], one_recv.at[1], beside)
    my = copy(meta_v, meta_in, one_send.at[2], one_recv.at[2], beside)
    for q in range(PIECES):
        bxs[q].start()
        for move in hops(0):
            guarded(move[2], lambda move=move, q=q: az(0, move, q).start())
        ax(0, q).start()
    my.start()
    vy.start()
    for lay in lays:
        lay.wait()
    for bx in bxs:
        bx.wait_recv()

    def second_own(k):
        for move, turn in zip(hops(0), (z, depth - 1 - z)):
            guarded(both(move[2], turn == k), lambda move=move: [bz(0, move, q).start() for q in range(PIECES)] and None)

    def forward(b, q):
        def run():
            az_wait(b, q)
            for move in hops(b):
                guarded(move[2], lambda move=move: az(b, move, q).start())
            ax(b, q).start()

        guarded(place(b)[1], run)

    def forward_second(b):
        def run():
            bz_wait(b)
            for move in hops(b):
                guarded(move[2], lambda move=move: [bz(b, move, q).start() for q in range(PIECES)] and None)

        guarded(place(b)[1], run)

    def steps(b):
        if b in (depth - 1, 2 * depth - 2):
            return [(pl.ds(q * chunk, chunk), chunk, (q,)) for q in range(PIECES)]
        return [(pl.ds(0, rows), rows, tuple(range(PIECES)))]

    def products(b, strip, stored, info, span, count, qs):
        zp = place(b)[0]

        def slot(s, carry):
            at_row = info[1, s]
            left = jnp.concatenate([bufs[b][q][side, at_row] for side in (0, 1) for q in qs], axis=0)
            new = jnp.dot(left, stored[info[0, s]], preferred_element_type=jnp.float32)
            runs[s + 1, : 2 * count] = new + runs[s, : 2 * count] * info[2, s].astype(jnp.float32)
            return carry

        runs[0] = jnp.zeros((2 * rows, size), jnp.float32)
        lax.fori_loop(0, slots, slot, 0, unroll=8)
        for c in range(col_blocks):
            value = runs[info[3, c] + 1, : 2 * count] * info[4, c].astype(jnp.float32)
            part[zp, strip, :, span, c * size:(c + 1) * size] = value.reshape(2, count, size)

    def core_copy(b, strip, i):
        zp, span = place(b)[0], steps(b)[i][0]
        return copy(part.at[zp, strip, :, span], core_in.at[zp % half, strip, :, span],
                    core_send.at[b, strip, i], core_recv.at[b, strip, i], twin)

    def target(b, i):
        return out.at[place(b)[0] % half * 2 + y, :, steps(b)[i][0]]

    def y_copy(b, i):
        return copy(y_out.at[place(b)[0] % half, :, steps(b)[i][0]], target(b, i), y_send.at[b, i], y_recv.at[b, i], beside)

    def own_copy(b, i):
        zp, span = place(b)[0], steps(b)[i][0]
        return pltpu.make_async_copy(own_out.at[zp % half, :, span], target(b, i), own_sem.at[b, i])

    def mine(b):
        return place(b)[0] // half == core

    def compute(b, i):
        span, count, qs = steps(b)[i]

        def run():
            ax_wait(b, qs)
            for strip, stored, info in ((0, v_other, meta_other), (1, v_own, meta)):
                products(b, strip, stored, info, span, count, qs)
                pl.when(jnp.logical_not(mine(b)))(lambda strip=strip: core_copy(b, strip, i).start())

        guarded(place(b)[1], run)

    def finish(b, i):
        def run():
            zp, span = place(b)[0], steps(b)[i][0]
            slot = zp % half
            core_copy(b, 0, i).wait_recv()
            y_out[slot, :, span] = part[zp, 0, :, span] + core_in[slot, 0, :, span]
            y_copy(b, i).start()
            core_copy(b, 1, i).wait_recv()
            own_out[slot, :, span] = part[zp, 1, :, span] + core_in[slot, 1, :, span]
            own_copy(b, i).start()

        guarded(both(place(b)[1], mine(b)), run)

    def at(k):
        return [0] if k == 0 else [k, depth - 1 + k]

    second_own(0)
    for k in range(1, depth):
        for q in range(PIECES):
            for b in at(k):
                forward(b, q)
        second_own(k)
    own_v.wait()
    own_m.wait()
    my.wait_recv()
    into = pltpu.make_async_copy(meta_in, meta_other, local_sem.at[2])
    into.start()
    into.wait()
    vy.wait_recv()
    waiting = [(0, 0)]
    compute(0, 0)
    for k in range(1, depth):
        for b in at(k):
            forward_second(b)
        for i in range(len(steps(k))):
            for todo in waiting:
                finish(*todo)
            waiting = [(b, i) for b in at(k)]
            for todo in waiting:
                compute(*todo)
    for todo in waiting:
        finish(*todo)

    for bx in bxs:
        bx.wait_send()
    vy.wait_send()
    my.wait_send()
    for b in range(2 * depth - 1):
        valid = place(b)[1]
        for move in hops(b):
            guarded(both(valid, move[2]), lambda b=b, move=move: [(az(b, move, q).wait_send(), bz(b, move, q).wait_send()) for q in range(PIECES)] and None)
        guarded(valid, lambda b=b: [ax(b, q).wait_send() for q in range(PIECES)] and None)
        other = jnp.logical_not(mine(b))
        for i in range(len(steps(b))):
            guarded(both(valid, other), lambda b=b, i=i: [core_copy(b, j, i).wait_send() for j in (0, 1)] and None)
            guarded(both(valid, mine(b)), lambda b=b, i=i: [y_copy(b, i).wait(), own_copy(b, i).wait()] and None)


def slot_table(places, count, col_blocks):
    total = places.shape[0]
    ids = jnp.arange(total, dtype=jnp.int32)
    cols = jnp.where(ids < count, places % col_blocks, col_blocks)
    key = cols * total + ids
    rank = jnp.sum((key[None, :] < key[:, None]).astype(jnp.int32), axis=1)
    hit = (rank[:, None] == ids[None, :]).astype(jnp.int32)
    order = jnp.sum(hit * ids[:, None], axis=0)
    row = jnp.sum(hit * (places // col_blocks)[:, None], axis=0)
    col = jnp.sum(hit * cols[:, None], axis=0)
    before = jnp.sum((rank[:, None] + 1 == ids[None, :]).astype(jnp.int32) * (cols + 1)[:, None], axis=0) - 1
    same = (col == before).astype(jnp.int32)
    each = jnp.arange(col_blocks, dtype=jnp.int32)
    last = jnp.sum((cols[None, :] <= each[:, None]).astype(jnp.int32), axis=1) - 1
    some = jnp.sum((cols[None, :] == each[:, None]).astype(jnp.int32), axis=1)
    lanes = -(-max(total, col_blocks) // 128) * 128

    def wide(a):
        return jnp.pad(a, (0, lanes - a.shape[0]))

    zero = jnp.zeros((lanes,), jnp.int32)
    return jnp.stack([wide(order), wide(row), wide(same), wide(jnp.maximum(last, 0)), wide(jnp.minimum(some, 1)), zero, zero, zero])


def ring_shards(width, wide_size, t_amps, v_blocks, block_pos, block_count):
    rows, columns = t_amps.shape
    slots, size = v_blocks.shape[2], v_blocks.shape[3]
    depth = wide_size // 4
    half, buffers = depth // 2, 2 * depth - 1
    strip = width // wide_size
    meta = slot_table(block_pos[0, 0], block_count[0, 0], strip // size)
    by_piece = jnp.transpose(t_amps.reshape(PIECES, rows // PIECES, columns // size, size), (0, 2, 1, 3))
    bf16, f32, i32 = jnp.bfloat16, jnp.float32, jnp.int32
    dma = pltpu.SemaphoreType.DMA
    out = pl.pallas_call(
        functools.partial(ladder_kernel, depth),
        out_shape=jax.ShapeDtypeStruct((half * 2, 2, rows, strip), f32),
        in_specs=[
            pl.BlockSpec(memory_space=pl.ANY),
            pl.BlockSpec(memory_space=pl.ANY),
            pl.BlockSpec(memory_space=pltpu.VMEM),
        ],
        out_specs=pl.BlockSpec(memory_space=pl.ANY),
        scratch_shapes=[pltpu.VMEM((2, columns // size, rows // PIECES, size), bf16)] * (buffers * PIECES) + [
            pltpu.VMEM((slots, size, size), bf16),
            pltpu.VMEM((slots, size, size), bf16),
            pltpu.VMEM(meta.shape, i32),
            pltpu.SMEM(meta.shape, i32),
            pltpu.SMEM(meta.shape, i32),
            pltpu.VMEM((slots + 1, 2 * rows, size), f32),
            pltpu.VMEM((depth, 2, 2, rows, strip), f32),
            pltpu.VMEM((half, 2, 2, rows, strip), f32),
            pltpu.VMEM((half, 2, rows, strip), f32),
            pltpu.VMEM((half, 2, rows, strip), f32),
            dma((buffers, PIECES)),
            dma((PIECES,)), dma((PIECES,)), dma((PIECES,)),
            dma((4,)),
            dma((2 * depth, PIECES)), dma((buffers, PIECES)),
            dma((2 * depth, PIECES)), dma((buffers, PIECES)),
            dma((buffers, PIECES)), dma((buffers, PIECES)),
            dma((3,)), dma((3,)),
            dma((buffers, 2, PIECES)), dma((buffers, 2, PIECES)),
            dma((buffers, PIECES)), dma((buffers, PIECES)),
        ],
        compiler_params=pltpu.CompilerParams(
            collective_id=0, has_side_effects=True, vmem_limit_bytes=36 * 1024 * 1024
        ),
    )(by_piece, v_blocks, meta)
    return out.reshape(half * 4 * rows, strip)


def solution(mesh):
    in_specs = (
        P("wide", "narrow"),
        P("narrow", "wide", None, None, None),
        P("narrow", "wide", None),
        P("narrow", "wide"),
    )
    out_specs = P("narrow", "wide")
    wide_size, narrow_size = mesh.shape["wide"], mesh.shape["narrow"]

    def program(t_amps, v_blocks, block_pos, block_count):
        width = t_amps.shape[1]
        if narrow_size == 2 and wide_size % 8 == 0:
            body = functools.partial(ring_shards, width, wide_size)
        else:
            body = functools.partial(dense_shards, width)
        run = jax.shard_map(body, mesh=mesh, in_specs=in_specs, out_specs=out_specs, check_vma=False)
        return run(t_amps, v_blocks, block_pos, block_count)

    return program
```

profile of v0, /device:TPU:1, one launch (start us, length us, event | category | flops | bytes accessed | tf_op | source)
XLA Modules:
  0.0 104.0 jit_solution(16848245787834434508)
XLA Ops:
  0.7 0.7 broadcast_add_fusion
  1.3 0.2 convert_reduce_fusion
  1.5 0.1 select_reduce_fusion.1
  1.7 0.1 convert_reduce_fusion.1
  1.9 0.0 copy-start
  1.9 1.6 %copy.7 = bf16[4,8,128,128]{3,2,1,0:T(8,128)(2,1)S(1)} copy(bf16[4,8,128,128]{3,1,2,0:T(8,128)(2,1)} %bitcast.38) | data formatting | bytes 2097152
  3.5 0.7 copy.9
  4.2 0.0 copy-done
  4.2 98.4 %shard_map.46 = f32[4,2,32,2048]{3,2,1,0:T(8,128)S(1)} custom-call(bf16[2,128,16,128]{3,2,1,0:T(8,128)(2,1)S(1)} %bitcast.36, bf16[1,1,64,128,128]{4,3,2,1,0:T(8,128)(2,1)S(1)} %copy-done, s32[8,128]{1,0:T(8,128)S(1)} %stack.31.meta_v), custom_call_target="tpu_custom_call" | custom-call | tf_op jit(solution)/shard_map/pallas_call | solution.py:307
  102.7 1.3 %copy.12 = f32[256,2048]{1,0:T(8,128)} copy(f32[256,2048]{1,0:T(8,128)S(1)} %bitcast.35) | data formatting | bytes 4194304
  (12 shorter events, 0.1 us)
Async XLA Ops:
  1.9 2.3 %copy-start = (bf16[1,1,64,128,128]{4,3,2,1,0:T(8,128)(2,1)S(1)}, bf16[1,1,64,128,128]{4,3,2,1,0:T(8,128)(2,1)}, u32[]{:S(2)}) copy-start(bf16[1,1,64,128,128]{4,3,2,1,0:T(8,128)(2,1)} %v_tile.1) | copy-start | bytes 6291460
where the time goes:
time: 104 us
  Pallas kernels  98.4 us (95%)
  local copies, waits for them, and re-layouts  3.67 us (4%)
  other arithmetic  1.12 us (1%)
    pallas_call x1, Pallas kernels, ring_shards(): pl.pallas_call(functools.partial(ladder_kernel, depth), out_shape=jax.Sha...  98.4 us
    unnamed x4, local copies, waits for them, and re-layouts  2.94 us

commit v1 on v0

v1 whole, which is shorter than its diff:
```python
import functools

import jax
import jax.numpy as jnp
from jax import lax
from jax.experimental import pallas as pl
from jax.experimental.pallas import tpu as pltpu
from jax.sharding import PartitionSpec as P

MESH = pl.DeviceIdType.MESH
PIECES = 4


def dense_shards(width, t_amps, v_blocks, block_pos, block_count):
    stored = v_blocks[0, 0]
    places = block_pos[0, 0]
    slot_count = block_count[0, 0]
    block_size = stored.shape[1]
    slot_total = stored.shape[0]
    row_blocks = t_amps.shape[1] // block_size
    col_blocks = width // (lax.axis_size("wide") * block_size)
    live_mask = (jnp.arange(slot_total, dtype=jnp.int32) < slot_count).astype(jnp.bfloat16)
    masked = stored * live_mask[:, None, None]
    dense_tile = jnp.zeros((row_blocks * col_blocks, block_size, block_size), jnp.bfloat16)
    dense_tile = dense_tile.at[places].add(masked)
    dense_tile = dense_tile.reshape(row_blocks, col_blocks, block_size, block_size)
    dense_tile = jnp.transpose(dense_tile, (0, 2, 1, 3)).reshape(row_blocks * block_size, col_blocks * block_size)
    gathered = lax.all_gather(t_amps, "wide", axis=0, tiled=True)
    partial_sum = jnp.dot(gathered, dense_tile, preferred_element_type=jnp.float32)
    return lax.psum_scatter(partial_sum, "narrow", scatter_dimension=0, tiled=True)


def ladder_kernel(depth, t, v_tile, meta_v, out, *scratch):
    held = scratch[: (2 * depth - 1) * PIECES]
    bufs = [held[b * PIECES:(b + 1) * PIECES] for b in range(2 * depth - 1)]
    (v_own, v_other, meta_in, meta, meta_other, runs, part, core_in, y_out, own_out,
     lay_sem, local_sem, z_send, z_recv, x_send, x_recv, one_send, one_recv, core_send, core_recv, y_send, y_recv,
     own_sem) = scratch[(2 * depth - 1) * PIECES:]
    wide, core = lax.axis_index("wide"), lax.axis_index("narrow")
    z, y, x = wide // 4, (wide // 2) % 2, wide % 2
    up, down = (wide + 4, core), (wide - 4, core)
    across = (wide + 1 - 2 * x, core)
    beside = (wide + 2 - 4 * y, core)
    twin = (wide, 1 - core)
    half = depth // 2
    pieces, row_blocks, chunk, unused = t.shape
    v = v_tile.at[0, 0]
    slots, size = v.shape[0], v.shape[1]
    col_blocks = out.shape[-1] // size
    has_up, has_down = z < depth - 1, z > 0
    at_end = jnp.logical_or(z == 0, z == depth - 1)
    even = tuple(range(0, pieces, 2))
    odd = tuple(range(1, pieces, 2))
    halves = pieces // 2

    def copy(src, dst, send, recv, device):
        return pltpu.make_async_remote_copy(
            src_ref=src, dst_ref=dst, send_sem=send, recv_sem=recv, device_id=device, device_id_type=MESH
        )

    def guarded(cond, fn):
        if cond is None:
            fn()
        else:
            pl.when(cond)(fn)

    def both(a, b):
        return b if a is None else a if b is None else jnp.logical_and(a, b)

    def shards(k):
        if k == 0:
            return [(0, z, None, None)]
        return [(k, z - k, z >= k, 0), (depth - 1 + k, z + k, z + k < depth, 1)]

    def is_end(k, way):
        return at_end if k == 0 else (z == k) if way == 0 else (z + k == depth - 1)

    def onward(b, way):
        ups = [] if way == 1 or b == depth - 1 else [(0, up, has_up, b + 1)]
        downs = [] if way == 0 or b == 2 * depth - 2 else [(1, down, has_down, depth if b == 0 else b + 1)]
        return ups + downs

    def z_copy(b, kind, q, move):
        side = x if kind == 0 else 1 - x
        direction, device, unused, landing = move
        return copy(bufs[b][q].at[side], bufs[landing][q].at[side], z_send.at[direction, b, kind, q], z_recv.at[landing, kind, q], device)

    def x_copy(b, q):
        ref = bufs[b][q].at[x]
        return copy(ref, ref, x_send.at[b, q], x_recv.at[b, q], across)

    def z_wait(b, kind, q):
        ref = bufs[b][q].at[x if kind == 0 else 1 - x]
        copy(ref, ref, z_send.at[0, b, kind, q], z_recv.at[b, kind, q], up).wait_recv()

    def x_wait(b, q):
        ref = bufs[b][q].at[1 - x]
        copy(ref, ref, x_send.at[b, q], x_recv.at[b, q], across).wait_recv()

    lays = [pltpu.make_async_copy(t.at[q], bufs[0][q].at[x], lay_sem.at[q]) for q in range(pieces)]
    own_v = pltpu.make_async_copy(v, v_own, local_sem.at[0])
    own_m = pltpu.make_async_copy(meta_v, meta, local_sem.at[1])
    for lay in lays:
        lay.start()
    own_v.start()
    own_m.start()
    barrier = pltpu.get_barrier_semaphore()
    for device in (across, beside, twin):
        pl.semaphore_signal(barrier, inc=1, device_id=device, device_id_type=MESH)
    pl.when(has_up)(lambda: pl.semaphore_signal(barrier, inc=1, device_id=up, device_id_type=MESH))
    pl.when(has_down)(lambda: pl.semaphore_signal(barrier, inc=1, device_id=down, device_id_type=MESH))
    for lay in lays:
        lay.wait()
    pl.semaphore_wait(barrier, 3 + has_up.astype(jnp.int32) + has_down.astype(jnp.int32))

    vy = copy(v, v_other, one_send.at[0], one_recv.at[0], beside)
    my = copy(meta_v, meta_in, one_send.at[1], one_recv.at[1], beside)
    for qz, qx in zip(even + odd, odd + even):
        for move in onward(0, None):
            guarded(move[2], lambda move=move: z_copy(0, 0, qz, move).start())
        x_copy(0, qx).start()
    my.start()
    vy.start()

    def relay(k, kind, q):
        for b, zp, valid, way in shards(k):
            def run(b=b, way=way):
                z_wait(b, kind, q)
                for move in onward(b, way):
                    guarded(move[2], lambda move=move: z_copy(b, kind, q, move).start())
                if kind == 0:
                    if q in even:
                        x_copy(b, q).start()
                    else:
                        pl.when(jnp.logical_not(is_end(k, way)))(lambda: x_copy(b, q).start())

            guarded(valid if kind == 0 else both(valid, is_end(k, way)), run)

    def relay_own(q):
        x_wait(0, q)

        def run():
            for move in onward(0, None):
                guarded(move[2], lambda move=move: z_copy(0, 1, q, move).start())

        pl.when(at_end)(run)

    def span(h):
        return pl.ds(2 * h * chunk, 2 * chunk)

    def core_copy(zp, strip, h):
        return copy(part.at[zp, strip, :, span(h)], core_in.at[zp % half, strip, :, span(h)],
                    core_send.at[zp, strip, h], core_recv.at[zp, strip, h], twin)

    def target(zp, h):
        return out.at[zp % half * 2 + y, :, span(h)]

    def y_copy(zp, h):
        return copy(y_out.at[zp % half, :, span(h)], target(zp, h), y_send.at[zp, h], y_recv.at[zp, h], beside)

    def own_copy(zp, h):
        return pltpu.make_async_copy(own_out.at[zp % half, :, span(h)], target(zp, h), own_sem.at[zp, h])

    def mine(zp):
        return zp // half == core

    strips = ((v_other, meta_other), (v_own, meta))

    def products(b, zp, h):
        def slot(s, carry):
            for strip, (stored, info) in enumerate(strips):
                at_row = info[1, s]
                left = jnp.concatenate([bufs[b][q][side, at_row] for side in (0, 1) for q in (2 * h, 2 * h + 1)], axis=0)
                new = jnp.dot(left, stored[info[0, s]], preferred_element_type=jnp.float32)
                runs[strip, s + 1] = new + runs[strip, s] * info[2, s].astype(jnp.float32)
            return carry

        lax.fori_loop(0, slots, slot, 0, unroll=8)
        for strip, (stored, info) in enumerate(strips):
            for c in range(col_blocks):
                value = runs[strip, info[3, c] + 1] * info[4, c].astype(jnp.float32)
                part[zp, strip, :, span(h), c * size:(c + 1) * size] = value.reshape(2, 2 * chunk, size)
            pl.when(jnp.logical_not(mine(zp)))(lambda: core_copy(zp, strip, h).start())

    def compute(k, h):
        for b, zp, valid, way in shards(k):
            def run(b=b, zp=zp, way=way):
                x_wait(b, 2 * h)
                if k == depth - 1:
                    z_wait(b, 1, 2 * h + 1)
                elif k > 0:
                    pl.when(jnp.logical_not(is_end(k, way)))(lambda: x_wait(b, 2 * h + 1))
                products(b, zp, h)

            guarded(valid, run)

    def finish(k, h):
        for b, zp, valid, way in shards(k):
            def run(zp=zp):
                core_copy(zp, 0, h).wait_recv()
                y_out[zp % half, :, span(h)] = part[zp, 0, :, span(h)] + core_in[zp % half, 0, :, span(h)]
                y_copy(zp, h).start()
                core_copy(zp, 1, h).wait_recv()
                own_out[zp % half, :, span(h)] = part[zp, 1, :, span(h)] + core_in[zp % half, 1, :, span(h)]
                own_copy(zp, h).start()

            guarded(both(valid, mine(zp)), run)

    for strip in (0, 1):
        runs[strip, 0] = jnp.zeros(runs.shape[2:], jnp.float32)
    for q in even:
        relay(1, 0, q)
    for q in odd:
        relay_own(q)
    for q in odd:
        relay(1, 0, q)
    for k in range(2, depth - 1):
        for qk, ql in zip(even, odd):
            relay(k, 0, qk)
            relay(k - 1, 1, ql)
        for q in odd:
            relay(k, 0, q)
    own_v.wait()
    own_m.wait()
    my.wait_recv()
    into = pltpu.make_async_copy(meta_in, meta_other, local_sem.at[2])
    into.start()
    into.wait()
    vy.wait_recv()
    compute(0, 0)
    compute(0, 1)
    finish(0, 0)
    for q in odd:
        relay(depth - 2, 1, q)
    waiting = [(0, 1)]
    for k in range(1, depth):
        if k == depth - 2:
            for q in even + odd:
                relay(depth - 1, 0, q)
        for h in range(halves):
            compute(k, h)
            for todo in waiting:
                finish(*todo)
            waiting = [(k, h)]
    for todo in waiting:
        finish(*todo)

    vy.wait_send()
    my.wait_send()
    for k in range(depth):
        for b, zp, valid, way in shards(k):
            def run(b=b, zp=zp, way=way):
                for move in onward(b, way):
                    guarded(move[2], lambda move=move: [z_copy(b, 0, q, move).wait_send() for q in range(pieces)] and None)
                    guarded(both(is_end(k, way), move[2]), lambda move=move: [z_copy(b, 1, q, move).wait_send() for q in odd] and None)
                for q in even:
                    x_copy(b, q).wait_send()
                guarded(None if k == 0 else jnp.logical_not(is_end(k, way)), lambda: [x_copy(b, q).wait_send() for q in odd] and None)
                other = jnp.logical_not(mine(zp))
                pl.when(other)(lambda: [core_copy(zp, j, h).wait_send() for j in (0, 1) for h in range(halves)] and None)
                pl.when(mine(zp))(lambda: [(y_copy(zp, h).wait(), own_copy(zp, h).wait()) for h in range(halves)] and None)

            guarded(valid, run)


def slot_table(places, count, col_blocks):
    total = places.shape[0]
    ids = jnp.arange(total, dtype=jnp.int32)
    cols = jnp.where(ids < count, places % col_blocks, col_blocks)
    key = cols * total + ids
    rank = jnp.sum((key[None, :] < key[:, None]).astype(jnp.int32), axis=1)
    hit = (rank[:, None] == ids[None, :]).astype(jnp.int32)
    order = jnp.sum(hit * ids[:, None], axis=0)
    row = jnp.sum(hit * (places // col_blocks)[:, None], axis=0)
    col = jnp.sum(hit * cols[:, None], axis=0)
    before = jnp.sum((rank[:, None] + 1 == ids[None, :]).astype(jnp.int32) * (cols + 1)[:, None], axis=0) - 1
    same = (col == before).astype(jnp.int32)
    each = jnp.arange(col_blocks, dtype=jnp.int32)
    last = jnp.sum((cols[None, :] <= each[:, None]).astype(jnp.int32), axis=1) - 1
    some = jnp.sum((cols[None, :] == each[:, None]).astype(jnp.int32), axis=1)
    lanes = -(-max(total, col_blocks) // 128) * 128

    def wide(a):
        return jnp.pad(a, (0, lanes - a.shape[0]))

    zero = jnp.zeros((lanes,), jnp.int32)
    return jnp.stack([wide(order), wide(row), wide(same), wide(jnp.maximum(last, 0)), wide(jnp.minimum(some, 1)), zero, zero, zero])


def ring_shards(width, wide_size, t_amps, v_blocks, block_pos, block_count):
    rows, columns = t_amps.shape
    slots, size = v_blocks.shape[2], v_blocks.shape[3]
    depth = wide_size // 4
    half, buffers = depth // 2, 2 * depth - 1
    strip = width // wide_size
    chunk = rows // PIECES
    meta = slot_table(block_pos[0, 0], block_count[0, 0], strip // size)
    by_piece = jnp.transpose(t_amps.reshape(PIECES, chunk, columns // size, size), (0, 2, 1, 3))
    bf16, f32, i32 = jnp.bfloat16, jnp.float32, jnp.int32
    dma = pltpu.SemaphoreType.DMA
    out = pl.pallas_call(
        functools.partial(ladder_kernel, depth),
        out_shape=jax.ShapeDtypeStruct((half * 2, 2, rows, strip), f32),
        in_specs=[
            pl.BlockSpec(memory_space=pltpu.HBM),
            pl.BlockSpec(memory_space=pltpu.HBM),
            pl.BlockSpec(memory_space=pltpu.VMEM),
        ],
        out_specs=pl.BlockSpec(memory_space=pl.ANY),
        scratch_shapes=[pltpu.VMEM((2, columns // size, chunk, size), bf16)] * (buffers * PIECES) + [
            pltpu.VMEM((slots, size, size), bf16),
            pltpu.VMEM((slots, size, size), bf16),
            pltpu.VMEM(meta.shape, i32),
            pltpu.SMEM(meta.shape, i32),
            pltpu.SMEM(meta.shape, i32),
            pltpu.VMEM((2, slots + 1, 4 * chunk, size), f32),
            pltpu.VMEM((depth, 2, 2, rows, strip), f32),
            pltpu.VMEM((half, 2, 2, rows, strip), f32),
            pltpu.VMEM((half, 2, rows, strip), f32),
            pltpu.VMEM((half, 2, rows, strip), f32),
            dma((PIECES,)),
            dma((3,)),
            dma((2, buffers, 2, PIECES)), dma((buffers, 2, PIECES)),
            dma((buffers, PIECES)), dma((buffers, PIECES)),
            dma((2,)), dma((2,)),
            dma((depth, 2, PIECES // 2)), dma((depth, 2, PIECES // 2)),
            dma((depth, PIECES // 2)), dma((depth, PIECES // 2)),
            dma((depth, PIECES // 2)),
        ],
        compiler_params=pltpu.CompilerParams(
            collective_id=0, has_side_effects=True, vmem_limit_bytes=36 * 1024 * 1024
        ),
    )(by_piece, v_blocks, meta)
    return out.reshape(half * 4 * rows, strip)


def solution(mesh):
    in_specs = (
        P("wide", "narrow"),
        P("narrow", "wide", None, None, None),
        P("narrow", "wide", None),
        P("narrow", "wide"),
    )
    out_specs = P("narrow", "wide")
    wide_size, narrow_size = mesh.shape["wide"], mesh.shape["narrow"]

    def program(t_amps, v_blocks, block_pos, block_count):
        width = t_amps.shape[1]
        if narrow_size == 2 and wide_size >= 16 and wide_size % 8 == 0:
            body = functools.partial(ring_shards, width, wide_size)
        else:
            body = functools.partial(dense_shards, width)
        run = jax.shard_map(body, mesh=mesh, in_specs=in_specs, out_specs=out_specs, check_vma=False)
        return run(t_amps, v_blocks, block_pos, block_count)

    return program
```

time: 104 us -> 101 us (0.971)
  Pallas kernels: 98.4 us -> 95 us
    pallas_call x1, Pallas kernels: 98.4 us -> 95 us  [ring_shards(): pl.pallas_call(functools.partial(ladder_kernel, depth), out_shape=jax.Sha...]
    unnamed x4 -> x5, local copies, waits for them, and re-layouts: 2.94 us -> 4.13 us
where the time goes in v1:
time: 101 us
  Pallas kernels  95 us (94%)
  local copies, waits for them, and re-layouts  4.18 us (4%)
  other arithmetic  1.12 us (1%)
    pallas_call x1, Pallas kernels, ring_shards(): pl.pallas_call(functools.partial(ladder_kernel, depth), out_shape=jax.Sha...  95 us
    unnamed x5, local copies, waits for them, and re-layouts  4.13 us

profile of v1, /device:TPU:1, one launch (start us, length us, event | category | flops | bytes accessed | tf_op | source)
XLA Modules:
  0.0 101.0 jit_solution(7917207365988599731)
XLA Ops:
  0.7 0.7 broadcast_add_fusion
  1.3 0.2 convert_reduce_fusion
  1.5 0.1 select_reduce_fusion.1
  1.7 0.1 convert_reduce_fusion.1
  1.9 0.0 copy-start
  1.9 1.6 %copy-done = bf16[1,1,64,128,128]{4,3,2,1,0:T(8,128)(2,1)S(1)} copy-done((bf16[1,1,64,128,128]{4,3,2,1,0:T(8,128)(2,1)S(1)}, bf16[1,1,64,128,128]{4,3,2,1,0:T(8,128)(2,1)}, u32[]{:S(2)}) %copy-start) | copy-done | bytes 2097176
  3.5 0.0 copy-start.1
  3.5 1.2 %copy-done.1 = bf16[32,16384]{1,0:T(8,128)(2,1)S(1)} copy-done((bf16[32,16384]{1,0:T(8,128)(2,1)S(1)}, bf16[32,16384]{1,0:T(8,128)(2,1)}, u32[]{:S(2)}) %copy-start.1) | copy-done | bytes 1048600
  4.7 95.0 %shard_map.46 = f32[4,2,32,2048]{3,2,1,0:T(8,128)S(1)} custom-call(bf16[4,128,8,128]{3,2,1,0:T(8,128)(2,1)S(1)} %bitcast.33, bf16[1,1,64,128,128]{4,3,2,1,0:T(8,128)(2,1)S(1)} %copy-done, s32[8,128]{1,0:T(8,128)S(1)} %stack.31.meta_v), custom_call_target="tpu_custom_call" | custom-call | tf_op jit(solution)/shard_map/pallas_call | solution.py:301
  99.7 1.3 %copy.7 = f32[256,2048]{1,0:T(8,128)} copy(f32[256,2048]{1,0:T(8,128)S(1)} %bitcast.32) | data formatting | bytes 4194304
  (12 shorter events, 0.1 us)
Async XLA Ops:
  1.9 1.6 %copy-start = (bf16[1,1,64,128,128]{4,3,2,1,0:T(8,128)(2,1)S(1)}, bf16[1,1,64,128,128]{4,3,2,1,0:T(8,128)(2,1)}, u32[]{:S(2)}) copy-start(bf16[1,1,64,128,128]{4,3,2,1,0:T(8,128)(2,1)} %v_tile.1) | copy-start | bytes 6291460
  3.5 1.2 %copy-start.1 = (bf16[32,16384]{1,0:T(8,128)(2,1)S(1)}, bf16[32,16384]{1,0:T(8,128)(2,1)}, u32[]{:S(2)}) copy-start(bf16[32,16384]{1,0:T(8,128)(2,1)} %param.4) | copy-start | bytes 3145732

commit v2 on v1

--- a/solution.py
+++ b/solution.py
@@ -49,9 +49,8 @@
     col_blocks = out.shape[-1] // size
     has_up, has_down = z < depth - 1, z > 0
     at_end = jnp.logical_or(z == 0, z == depth - 1)
-    even = tuple(range(0, pieces, 2))
-    odd = tuple(range(1, pieces, 2))
-    halves = pieces // 2
+    first = row_blocks // 2
+    second_cols = pl.ds(first, row_blocks - first)
 
     def copy(src, dst, send, recv, device):
         return pltpu.make_async_remote_copy(
@@ -80,22 +79,35 @@
         downs = [] if way == 0 or b == 2 * depth - 2 else [(1, down, has_down, depth if b == 0 else b + 1)]
         return ups + downs
 
+    def z_ref(b, kind, q):
+        return bufs[b][q].at[x] if kind == 0 else bufs[b][q].at[1 - x, second_cols]
+
     def z_copy(b, kind, q, move):
-        side = x if kind == 0 else 1 - x
         direction, device, unused, landing = move
-        return copy(bufs[b][q].at[side], bufs[landing][q].at[side], z_send.at[direction, b, kind, q], z_recv.at[landing, kind, q], device)
-
-    def x_copy(b, q):
-        ref = bufs[b][q].at[x]
+        return copy(z_ref(b, kind, q), z_ref(landing, kind, q), z_send.at[direction, b, kind, q], z_recv.at[landing, kind, q], device)
+
+    def x_copy(b, q, cols, side):
+        ref = bufs[b][q].at[side, pl.ds(0, cols)]
         return copy(ref, ref, x_send.at[b, q], x_recv.at[b, q], across)
 
     def z_wait(b, kind, q):
-        ref = bufs[b][q].at[x if kind == 0 else 1 - x]
+        ref = z_ref(b, kind, q)
         copy(ref, ref, z_send.at[0, b, kind, q], z_recv.at[b, kind, q], up).wait_recv()
 
-    def x_wait(b, q):
-        ref = bufs[b][q].at[1 - x]
-        copy(ref, ref, x_send.at[b, q], x_recv.at[b, q], across).wait_recv()
+    def crossing(k, way, fn):
+        if k == 0:
+            fn(row_blocks)
+        elif k == depth - 1:
+            fn(first)
+        else:
+            pl.when(is_end(k, way))(lambda: fn(first))
+            pl.when(jnp.logical_not(is_end(k, way)))(lambda: fn(row_blocks))
+
+    def x_start(k, b, way, q):
+        crossing(k, way, lambda cols: x_copy(b, q, cols, x).start())
+
+    def x_wait(k, b, way, q):
+        crossing(k, way, lambda cols: x_copy(b, q, cols, 1 - x).wait_recv())
 
     lays = [pltpu.make_async_copy(t.at[q], bufs[0][q].at[x], lay_sem.at[q]) for q in range(pieces)]
     own_v = pltpu.make_async_copy(v, v_own, local_sem.at[0])
@@ -115,10 +127,10 @@
 
     vy = copy(v, v_other, one_send.at[0], one_recv.at[0], beside)
     my = copy(meta_v, meta_in, one_send.at[1], one_recv.at[1], beside)
-    for qz, qx in zip(even + odd, odd + even):
+    for q in range(pieces):
         for move in onward(0, None):
-            guarded(move[2], lambda move=move: z_copy(0, 0, qz, move).start())
-        x_copy(0, qx).start()
+            guarded(move[2], lambda move=move: z_copy(0, 0, q, move).start())
+        x_start(0, 0, None, q)
     my.start()
     vy.start()
 
@@ -129,15 +141,12 @@
                 for move in onward(b, way):
                     guarded(move[2], lambda move=move: z_copy(b, kind, q, move).start())
                 if kind == 0:
-                    if q in even:
-                        x_copy(b, q).start()
-                    else:
-                        pl.when(jnp.logical_not(is_end(k, way)))(lambda: x_copy(b, q).start())
+                    x_start(k, b, way, q)
 
             guarded(valid if kind == 0 else both(valid, is_end(k, way)), run)
 
     def relay_own(q):
-        x_wait(0, q)
+        x_wait(0, 0, None, q)
 
         def run():
             for move in onward(0, None):
@@ -145,80 +154,91 @@
 
         pl.when(at_end)(run)
 
-    def span(h):
-        return pl.ds(2 * h * chunk, 2 * chunk)
-
-    def core_copy(zp, strip, h):
-        return copy(part.at[zp, strip, :, span(h)], core_in.at[zp % half, strip, :, span(h)],
-                    core_send.at[zp, strip, h], core_recv.at[zp, strip, h], twin)
-
-    def target(zp, h):
-        return out.at[zp % half * 2 + y, :, span(h)]
-
-    def y_copy(zp, h):
-        return copy(y_out.at[zp % half, :, span(h)], target(zp, h), y_send.at[zp, h], y_recv.at[zp, h], beside)
-
-    def own_copy(zp, h):
-        return pltpu.make_async_copy(own_out.at[zp % half, :, span(h)], target(zp, h), own_sem.at[zp, h])
+    def groups(k):
+        count = 1 if k == depth - 1 else 2
+        return [(q, count) for q in range(0, pieces, count)]
+
+    def span(g):
+        return pl.ds(g[0] * chunk, g[1] * chunk)
+
+    def core_copy(zp, strip, g):
+        return copy(part.at[zp, strip, :, span(g)], core_in.at[zp % half, strip, :, span(g)],
+                    core_send.at[zp, strip, g[0]], core_recv.at[zp, strip, g[0]], twin)
+
+    def target(zp, g):
+        return out.at[zp % half * 2 + y, :, span(g)]
+
+    def y_copy(zp, g):
+        return copy(y_out.at[zp % half, :, span(g)], target(zp, g), y_send.at[zp, g[0]], y_recv.at[zp, g[0]], beside)
+
+    def own_copy(zp, g):
+        return pltpu.make_async_copy(own_out.at[zp % half, :, span(g)], target(zp, g), own_sem.at[zp, g[0]])
 
     def mine(zp):
         return zp // half == core
 
-    strips = ((v_other, meta_other), (v_own, meta))
-
-    def products(b, zp, h):
+    tables = ((v_other, meta_other), (v_own, meta))
+
+    def products(b, zp, g, strips, unroll):
+        lines = 2 * g[1] * chunk
+
         def slot(s, carry):
-            for strip, (stored, info) in enumerate(strips):
+            for strip in strips:
+                stored, info = tables[strip]
                 at_row = info[1, s]
-                left = jnp.concatenate([bufs[b][q][side, at_row] for side in (0, 1) for q in (2 * h, 2 * h + 1)], axis=0)
+                left = jnp.concatenate([bufs[b][q][side, at_row] for side in (0, 1) for q in range(g[0], g[0] + g[1])], axis=0)
                 new = jnp.dot(left, stored[info[0, s]], preferred_element_type=jnp.float32)
-                runs[strip, s + 1] = new + runs[strip, s] * info[2, s].astype(jnp.float32)
+                runs[strip, s + 1, :lines] = new + runs[strip, s, :lines] * info[2, s].astype(jnp.float32)
             return carry
 
-        lax.fori_loop(0, slots, slot, 0, unroll=8)
-        for strip, (stored, info) in enumerate(strips):
+        lax.fori_loop(0, slots, slot, 0, unroll=unroll)
+        for strip in strips:
+            info = tables[strip][1]
             for c in range(col_blocks):
-                value = runs[strip, info[3, c] + 1] * info[4, c].astype(jnp.float32)
-                part[zp, strip, :, span(h), c * size:(c + 1) * size] = value.reshape(2, 2 * chunk, size)
-            pl.when(jnp.logical_not(mine(zp)))(lambda: core_copy(zp, strip, h).start())
-
-    def compute(k, h):
+                value = runs[strip, info[3, c] + 1, :lines] * info[4, c].astype(jnp.float32)
+                part[zp, strip, :, span(g), c * size:(c + 1) * size] = value.reshape(2, g[1] * chunk, size)
+            pl.when(jnp.logical_not(mine(zp)))(lambda: core_copy(zp, strip, g).start())
+
+    def compute(k, g, ahead=None):
         for b, zp, valid, way in shards(k):
             def run(b=b, zp=zp, way=way):
-                x_wait(b, 2 * h)
-                if k == depth - 1:
-                    z_wait(b, 1, 2 * h + 1)
-                elif k > 0:
-                    pl.when(jnp.logical_not(is_end(k, way)))(lambda: x_wait(b, 2 * h + 1))
-                products(b, zp, h)
+                for q in range(g[0], g[0] + g[1]):
+                    if k > 0:
+                        x_wait(k, b, way, q)
+                    if k == depth - 1:
+                        z_wait(b, 1, q)
+                if ahead is None:
+                    products(b, zp, g, (0, 1), 16)
+                else:
+                    products(b, zp, g, (0,), 32)
+                    finish(k, ahead, b)
+                    products(b, zp, g, (1,), 32)
 
             guarded(valid, run)
 
-    def finish(k, h):
+    def finish(k, g, only=None):
         for b, zp, valid, way in shards(k):
             def run(zp=zp):
-                core_copy(zp, 0, h).wait_recv()
-                y_out[zp % half, :, span(h)] = part[zp, 0, :, span(h)] + core_in[zp % half, 0, :, span(h)]
-                y_copy(zp, h).start()
-                core_copy(zp, 1, h).wait_recv()
-                own_out[zp % half, :, span(h)] = part[zp, 1, :, span(h)] + core_in[zp % half, 1, :, span(h)]
-                own_copy(zp, h).start()
-
-            guarded(both(valid, mine(zp)), run)
+                core_copy(zp, 0, g).wait_recv()
+                y_out[zp % half, :, span(g)] = part[zp, 0, :, span(g)] + core_in[zp % half, 0, :, span(g)]
+                y_copy(zp, g).start()
+                core_copy(zp, 1, g).wait_recv()
+                own_out[zp % half, :, span(g)] = part[zp, 1, :, span(g)] + core_in[zp % half, 1, :, span(g)]
+                own_copy(zp, g).start()
+
+            if only is None:
+                guarded(both(valid, mine(zp)), run)
+            elif only == b:
+                pl.when(mine(zp))(run)
 
     for strip in (0, 1):
         runs[strip, 0] = jnp.zeros(runs.shape[2:], jnp.float32)
-    for q in even:
+    for q in range(pieces):
         relay(1, 0, q)
-    for q in odd:
         relay_own(q)
-    for q in odd:
-        relay(1, 0, q)
     for k in range(2, depth - 1):
-        for qk, ql in zip(even, odd):
-            relay(k, 0, qk)
-            relay(k - 1, 1, ql)
-        for q in odd:
+        for q in range(pieces):
+            relay(k - 1, 1, q)
             relay(k, 0, q)
     own_v.wait()
     own_m.wait()
@@ -227,23 +247,31 @@
     into.start()
     into.wait()
     vy.wait_recv()
-    compute(0, 0)
-    compute(0, 1)
-    finish(0, 0)
-    for q in odd:
+    for g in groups(0):
+        compute(0, g)
+    finish(0, groups(0)[0])
+    compute(1, groups(1)[0])
+    finish(0, groups(0)[1])
+    for q in range(pieces):
         relay(depth - 2, 1, q)
-    waiting = [(0, 1)]
-    for k in range(1, depth):
-        if k == depth - 2:
-            for q in even + odd:
-                relay(depth - 1, 0, q)
-        for h in range(halves):
-            compute(k, h)
-            for todo in waiting:
-                finish(*todo)
-            waiting = [(k, h)]
-    for todo in waiting:
-        finish(*todo)
+    compute(1, groups(1)[1])
+    finish(1, groups(1)[0])
+    finish(1, groups(1)[1])
+    for k in range(2, depth - 1):
+        for n, g in enumerate(groups(k)):
+            if k == depth - 2:
+                for q in range(2 * n, 2 * n + 2):
+                    relay(depth - 1, 0, q)
+            compute(k, g)
+            finish(k, g)
+    ahead = None
+    for g in groups(depth - 1):
+        last = g[0] == pieces - 1
+        compute(depth - 1, g, ahead if last else None)
+        if ahead is not None and not last:
+            finish(depth - 1, ahead)
+        ahead = g
+    finish(depth - 1, ahead)
 
     vy.wait_send()
     my.wait_send()
@@ -252,13 +280,11 @@
             def run(b=b, zp=zp, way=way):
                 for move in onward(b, way):
                     guarded(move[2], lambda move=move: [z_copy(b, 0, q, move).wait_send() for q in range(pieces)] and None)
-                    guarded(both(is_end(k, way), move[2]), lambda move=move: [z_copy(b, 1, q, move).wait_send() for q in odd] and None)
-                for q in even:
-                    x_copy(b, q).wait_send()
-                guarded(None if k == 0 else jnp.logical_not(is_end(k, way)), lambda: [x_copy(b, q).wait_send() for q in odd] and None)
+                    guarded(both(is_end(k, way), move[2]), lambda move=move: [z_copy(b, 1, q, move).wait_send() for q in range(pieces)] and None)
+                crossing(k, way, lambda cols: [x_copy(b, q, cols, x).wait_send() for q in range(pieces)] and None)
                 other = jnp.logical_not(mine(zp))
-                pl.when(other)(lambda: [core_copy(zp, j, h).wait_send() for j in (0, 1) for h in range(halves)] and None)
-                pl.when(mine(zp))(lambda: [(y_copy(zp, h).wait(), own_copy(zp, h).wait()) for h in range(halves)] and None)
+                pl.when(other)(lambda: [core_copy(zp, j, g).wait_send() for j in (0, 1) for g in groups(k)] and None)
+                pl.when(mine(zp))(lambda: [(y_copy(zp, g).wait(), own_copy(zp, g).wait()) for g in groups(k)] and None)
 
             guarded(valid, run)
 
@@ -323,14 +349,14 @@
             dma((2, buffers, 2, PIECES)), dma((buffers, 2, PIECES)),
             dma((buffers, PIECES)), dma((buffers, PIECES)),
             dma((2,)), dma((2,)),
-            dma((depth, 2, PIECES // 2)), dma((depth, 2, PIECES // 2)),
-            dma((depth, PIECES // 2)), dma((depth, PIECES // 2)),
-            dma((depth, PIECES // 2)),
+            dma((depth, 2, PIECES)), dma((depth, 2, PIECES)),
+            dma((depth, PIECES)), dma((depth, PIECES)),
+            dma((depth, PIECES)),
         ],
         compiler_params=pltpu.CompilerParams(
-            collective_id=0, has_side_effects=True, vmem_limit_bytes=36 * 1024 * 1024
+            collective_id=0, has_side_effects=True, vmem_limit_bytes=40 * 1024 * 1024
         ),
-    )(by_piece, v_blocks, meta)
+    )(pltpu.with_memory_space_constraint(by_piece, pltpu.HBM), pltpu.with_memory_space_constraint(v_blocks, pltpu.HBM), meta)
     return out.reshape(half * 4 * rows, strip)
 
 

time: 101 us -> 96.2 us (0.952)
  local copies, waits for them, and re-layouts: 4.18 us -> 1.37 us
  Pallas kernels: 95 us -> 92.8 us
    unnamed x5 -> x1, local copies, waits for them, and re-layouts: 4.13 us -> 1.32 us
    pallas_call x1, Pallas kernels: 95 us -> 92.8 us  [ring_shards(): pl.pallas_call(functools.partial(ladder_kernel, depth), out_shape=jax.Sha...]
where the time goes in v2:
time: 96.2 us; the launch traced here: 96 us
  Pallas kernels  92.8 us (96%)
  local copies, waits for them, and re-layouts  1.37 us (1%)
  other arithmetic  1.12 us (1%)
    pallas_call x1, Pallas kernels, ring_shards(): pl.pallas_call(functools.partial(ladder_kernel, depth), out_shape=jax.Sha...  92.8 us

profile of v2, /device:TPU:1, one launch (start us, length us, event | category | flops | bytes accessed | tf_op | source)
XLA Modules:
  0.0 96.0 jit_solution(7507570423585637478)
XLA Ops:
  0.7 0.7 broadcast_add_fusion
  1.3 0.2 convert_reduce_fusion
  1.5 0.1 select_reduce_fusion.1
  1.7 0.1 convert_reduce_fusion.1
  1.9 92.8 %shard_map.46 = f32[4,2,32,2048]{3,2,1,0:T(8,128)S(1)} custom-call(bf16[4,128,8,128]{3,2,1,0:T(8,128)(2,1)} %bitcast.33, bf16[1,1,64,128,128]{4,3,2,1,0:T(8,128)(2,1)} %v_tile.1, s32[8,128]{1,0:T(8,128)S(1)} %stack.31.meta_v), custom_call_target="tpu_custom_call" | custom-call | tf_op jit(solution)/shard_map/pallas_call | solution.py:327
  94.7 1.3 %copy.7 = f32[256,2048]{1,0:T(8,128)} copy(f32[256,2048]{1,0:T(8,128)S(1)} %bitcast.32) | data formatting | bytes 4194304
  (12 shorter events, 0.1 us)

commit v3 on v2

v3 whole, which is shorter than its diff:
```python
import functools

import jax
import jax.numpy as jnp
from jax import lax
from jax.experimental import pallas as pl
from jax.experimental.pallas import tpu as pltpu
from jax.sharding import PartitionSpec as P

MESH = pl.DeviceIdType.MESH
PIECES = 4


def dense_shards(width, t_amps, v_blocks, block_pos, block_count):
    stored = v_blocks[0, 0]
    places = block_pos[0, 0]
    slot_count = block_count[0, 0]
    block_size = stored.shape[1]
    slot_total = stored.shape[0]
    row_blocks = t_amps.shape[1] // block_size
    col_blocks = width // (lax.axis_size("wide") * block_size)
    live_mask = (jnp.arange(slot_total, dtype=jnp.int32) < slot_count).astype(jnp.bfloat16)
    masked = stored * live_mask[:, None, None]
    dense_tile = jnp.zeros((row_blocks * col_blocks, block_size, block_size), jnp.bfloat16)
    dense_tile = dense_tile.at[places].add(masked)
    dense_tile = dense_tile.reshape(row_blocks, col_blocks, block_size, block_size)
    dense_tile = jnp.transpose(dense_tile, (0, 2, 1, 3)).reshape(row_blocks * block_size, col_blocks * block_size)
    gathered = lax.all_gather(t_amps, "wide", axis=0, tiled=True)
    partial_sum = jnp.dot(gathered, dense_tile, preferred_element_type=jnp.float32)
    return lax.psum_scatter(partial_sum, "narrow", scatter_dimension=0, tiled=True)


def ladder_kernel(depth, t, v_tile, pos, count, out, *scratch):
    total = (2 * depth - 1) * PIECES * 2
    bufs = [[scratch[2 * (b * PIECES + q):2 * (b * PIECES + q) + 2] for q in range(PIECES)] for b in range(2 * depth - 1)]
    (v_own, v_other, pos_own, count_own, pos_other, count_other, made, info_own, info_other, runs, part, core_in, y_out, own_out,
     lay_sem, local_sem, z_send, z_recv, x_send, x_recv, one_send, one_recv, core_send, core_recv, y_send, y_recv,
     own_sem) = scratch[total:]
    wide, core = lax.axis_index("wide"), lax.axis_index("narrow")
    z, y, x = wide // 4, (wide // 2) % 2, wide % 2
    up, down = (wide + 4, core), (wide - 4, core)
    across = (wide + 1 - 2 * x, core)
    beside = (wide + 2 - 4 * y, core)
    twin = (wide, 1 - core)
    half = depth // 2
    pieces, row_blocks, chunk, unused = t.shape
    v = v_tile.at[0, 0]
    slots, size = v.shape[0], v.shape[1]
    col_blocks = out.shape[-1] // size
    has_up, has_down = z < depth - 1, z > 0
    at_end = jnp.logical_or(z == 0, z == depth - 1)
    first = row_blocks // 2
    second_cols = pl.ds(first, row_blocks - first)

    def copy(src, dst, send, recv, device):
        return pltpu.make_async_remote_copy(
            src_ref=src, dst_ref=dst, send_sem=send, recv_sem=recv, device_id=device, device_id_type=MESH
        )

    def guarded(cond, fn):
        if cond is None:
            fn()
        else:
            pl.when(cond)(fn)

    def both(a, b):
        return b if a is None else a if b is None else jnp.logical_and(a, b)

    def shards(k):
        if k == 0:
            return [(0, z, None, None)]
        return [(k, z - k, z >= k, 0), (depth - 1 + k, z + k, z + k < depth, 1)]

    def is_end(k, way):
        return at_end if k == 0 else (z == k) if way == 0 else (z + k == depth - 1)

    def onward(b, way):
        ups = [] if way == 1 or b == depth - 1 else [(0, up, has_up, b + 1)]
        downs = [] if way == 0 or b == 2 * depth - 2 else [(1, down, has_down, depth if b == 0 else b + 1)]
        return ups + downs

    def z_ref(b, kind, q):
        return bufs[b][q][0] if kind == 0 else bufs[b][q][1].at[second_cols]

    def z_copy(b, kind, q, move):
        direction, device, unused, landing = move
        return copy(z_ref(b, kind, q), z_ref(landing, kind, q), z_send.at[direction, b, kind, q], z_recv.at[landing, kind, q], device)

    def x_copy(b, q, cols):
        mine_side, other_side = (ref.at[pl.ds(0, cols)] for ref in bufs[b][q])
        return copy(mine_side, other_side, x_send.at[b, q], x_recv.at[b, q], across)

    def z_wait(b, kind, q):
        ref = z_ref(b, kind, q)
        copy(ref, ref, z_send.at[0, b, kind, q], z_recv.at[b, kind, q], up).wait_recv()

    def crossing(k, way, fn):
        if k == 0:
            fn(row_blocks)
        elif k == depth - 1:
            fn(first)
        else:
            pl.when(is_end(k, way))(lambda: fn(first))
            pl.when(jnp.logical_not(is_end(k, way)))(lambda: fn(row_blocks))

    def x_start(k, b, way, q):
        crossing(k, way, lambda cols: x_copy(b, q, cols).start())

    def x_wait(k, b, way, q):
        crossing(k, way, lambda cols: x_copy(b, q, cols).wait_recv())

    lays = [pltpu.make_async_copy(t.at[q], bufs[0][q][0], lay_sem.at[q]) for q in range(pieces)]
    own_v = pltpu.make_async_copy(v, v_own, local_sem.at[0])
    own_p = pltpu.make_async_copy(pos, pos_own, local_sem.at[1])
    own_c = pltpu.make_async_copy(count, count_own, local_sem.at[2])
    for lay in lays:
        lay.start()
    own_v.start()
    own_p.start()
    own_c.start()
    barrier = pltpu.get_barrier_semaphore()
    for device in (across, beside, twin):
        pl.semaphore_signal(barrier, inc=1, device_id=device, device_id_type=MESH)
    pl.when(has_up)(lambda: pl.semaphore_signal(barrier, inc=1, device_id=up, device_id_type=MESH))
    pl.when(has_down)(lambda: pl.semaphore_signal(barrier, inc=1, device_id=down, device_id_type=MESH))
    for lay in lays:
        lay.wait()
    pl.semaphore_wait(barrier, 3 + has_up.astype(jnp.int32) + has_down.astype(jnp.int32))

    vy = copy(v, v_other, one_send.at[0], one_recv.at[0], beside)
    py = copy(pos, pos_other, one_send.at[1], one_recv.at[1], beside)
    cy = copy(count, count_other, one_send.at[2], one_recv.at[2], beside)
    for q in range(pieces):
        for move in onward(0, None):
            guarded(move[2], lambda move=move: z_copy(0, 0, q, move).start())
        x_start(0, 0, None, q)
    py.start()
    cy.start()
    vy.start()

    def relay(k, kind, q):
        for b, zp, valid, way in shards(k):
            def run(b=b, way=way):
                z_wait(b, kind, q)
                for move in onward(b, way):
                    guarded(move[2], lambda move=move: z_copy(b, kind, q, move).start())
                if kind == 0:
                    x_start(k, b, way, q)

            guarded(valid if kind == 0 else both(valid, is_end(k, way)), run)

    def relay_own(q):
        x_wait(0, 0, None, q)

        def run():
            for move in onward(0, None):
                guarded(move[2], lambda move=move: z_copy(0, 1, q, move).start())

        pl.when(at_end)(run)

    def steps(k):
        if k == depth - 1:
            tail = [(1 - x, (1,), (0, 1))] + [(1 - x, (1,), (q,)) for q in range(2, pieces)]
            return [(x, (0,), tuple(range(pieces)))] + tail
        return [(pl.ds(0, 2), (0, 1), (q, q + 1)) for q in range(0, pieces, 2)]

    def span(k, n):
        sides, unused, qs = steps(k)[n]
        return sides, pl.ds(qs[0] * chunk, len(qs) * chunk)

    def core_copy(zp, strip, k, n):
        return copy(part.at[zp, strip, *span(k, n)], core_in.at[zp % half, strip, *span(k, n)],
                    core_send.at[zp, strip, n], core_recv.at[zp, strip, n], twin)

    def target(zp, k, n):
        return out.at[zp % half * 2 + y, *span(k, n)]

    def y_copy(zp, k, n):
        return copy(y_out.at[zp % half, *span(k, n)], target(zp, k, n), y_send.at[zp, n], y_recv.at[zp, n], beside)

    def own_copy(zp, k, n):
        return pltpu.make_async_copy(own_out.at[zp % half, *span(k, n)], target(zp, k, n), own_sem.at[zp, n])

    def mine(zp):
        return zp // half == core

    def chain(places, live, strip):
        place = places[0]
        shift = (col_blocks - 1).bit_length()
        row = place >> shift if col_blocks == 1 << shift else place // col_blocks
        along = jnp.broadcast_to(place - row * col_blocks, (slots, slots))
        down = along.T
        earlier = lax.broadcasted_iota(jnp.int32, (slots, slots), 0)
        at = lax.broadcasted_iota(jnp.int32, (slots, slots), 1)
        known = jnp.where(earlier < live[...], earlier + 1, 0)
        before = jnp.max(jnp.where(jnp.logical_and(down == along, earlier < at), known, 0), axis=0, keepdims=True)
        last = jnp.max(jnp.where(down == at, known, 0), axis=0, keepdims=True)
        for i, line in enumerate((row, before, last)):
            made[strip, i:i + 1, :slots] = line

    tables = ((v_other, info_other), (v_own, info_own))

    def products(b, zp, k, n, strips, unroll):
        unused, sides, qs = steps(k)[n]
        lines = len(sides) * len(qs) * chunk

        def slot(s, carry):
            for strip in strips:
                stored, info = tables[strip]
                at_row = info[0, s]
                left = jnp.concatenate([bufs[b][q][side][at_row] for side in sides for q in qs], axis=0)
                new = jnp.dot(left, stored[s], preferred_element_type=jnp.float32)
                runs[strip, s + 1, :lines] = new + runs[strip, info[1, s], :lines]
            return carry

        lax.fori_loop(0, slots, slot, 0, unroll=unroll)
        for strip in strips:
            info = tables[strip][1]
            for c in range(col_blocks):
                value = runs[strip, info[2, c], :lines]
                for i, side in enumerate(sides):
                    part[zp, strip, x if side == 0 else 1 - x, span(k, n)[1], c * size:(c + 1) * size] = (
                        value[i * len(qs) * chunk:(i + 1) * len(qs) * chunk])
            pl.when(jnp.logical_not(mine(zp)))(lambda: core_copy(zp, strip, k, n).start())

    def compute(k, n, ahead=None):
        for b, zp, valid, way in shards(k):
            def run(b=b, zp=zp, way=way):
                for q in steps(k)[n][2]:
                    if 0 < k < depth - 1 or n > 0 and k > 0:
                        x_wait(k, b, way, q)
                    if n > 0 and k == depth - 1:
                        z_wait(b, 1, q)
                if ahead is None:
                    products(b, zp, k, n, (0, 1), 16)
                else:
                    products(b, zp, k, n, (0,), 32)
                    finish(k, ahead, b)
                    products(b, zp, k, n, (1,), 32)

            guarded(valid, run)

    def finish(k, n, only=None):
        for b, zp, valid, way in shards(k):
            def run(zp=zp):
                core_copy(zp, 0, k, n).wait_recv()
                y_out[zp % half, *span(k, n)] = part[zp, 0, *span(k, n)] + core_in[zp % half, 0, *span(k, n)]
                y_copy(zp, k, n).start()
                core_copy(zp, 1, k, n).wait_recv()
                own_out[zp % half, *span(k, n)] = part[zp, 1, *span(k, n)] + core_in[zp % half, 1, *span(k, n)]
                own_copy(zp, k, n).start()

            if only is None:
                guarded(both(valid, mine(zp)), run)
            elif only == b:
                pl.when(mine(zp))(run)

    for strip in (0, 1):
        runs[strip, 0] = jnp.zeros(runs.shape[2:], jnp.float32)
    for q in range(pieces):
        relay(1, 0, q)
        relay_own(q)
    own_p.wait()
    own_c.wait()
    chain(pos_own, count_own, 1)
    py.wait_recv()
    cy.wait_recv()
    chain(pos_other, count_other, 0)
    for k in range(2, depth - 1):
        for q in range(pieces):
            relay(k - 1, 1, q)
            relay(k, 0, q)
    into = [pltpu.make_async_copy(made.at[strip], tables[strip][1], local_sem.at[3 + strip]) for strip in (0, 1)]
    for each in into:
        each.start()
    for each in into:
        each.wait()
    own_v.wait()
    vy.wait_recv()
    compute(0, 0)
    compute(0, 1)
    finish(0, 0)
    compute(1, 0)
    finish(0, 1)
    for q in range(pieces):
        relay(depth - 2, 1, q)
    compute(1, 1)
    finish(1, 0)
    finish(1, 1)
    for k in range(2, depth - 1):
        for n in range(len(steps(k))):
            if k == depth - 2:
                for q in range(2 * n, 2 * n + 2):
                    relay(depth - 1, 0, q)
            compute(k, n)
            if n == 0:
                finish(k, n)
    compute(depth - 1, 0)
    finish(depth - 2, 1)
    final = len(steps(depth - 1)) - 1
    for n in range(1, final):
        compute(depth - 1, n)
        finish(depth - 1, n - 1)
    compute(depth - 1, final, final - 1)
    finish(depth - 1, final)

    vy.wait_send()
    py.wait_send()
    cy.wait_send()
    for k in range(depth):
        for b, zp, valid, way in shards(k):
            def run(b=b, zp=zp, way=way):
                for move in onward(b, way):
                    guarded(move[2], lambda move=move: [z_copy(b, 0, q, move).wait_send() for q in range(pieces)] and None)
                    guarded(both(is_end(k, way), move[2]), lambda move=move: [z_copy(b, 1, q, move).wait_send() for q in range(pieces)] and None)
                crossing(k, way, lambda cols: [x_copy(b, q, cols).wait_send() for q in range(pieces)] and None)
                other = jnp.logical_not(mine(zp))
                pl.when(other)(lambda: [core_copy(zp, j, k, n).wait_send() for j in (0, 1) for n in range(len(steps(k)))] and None)
                pl.when(mine(zp))(lambda: [(y_copy(zp, k, n).wait(), own_copy(zp, k, n).wait()) for n in range(len(steps(k)))] and None)

            guarded(valid, run)


def ring_shards(width, wide_size, t_amps, v_blocks, block_pos, block_count):
    rows, columns = t_amps.shape
    slots, size = v_blocks.shape[2], v_blocks.shape[3]
    depth = wide_size // 4
    half, buffers = depth // 2, 2 * depth - 1
    strip = width // wide_size
    chunk = rows // PIECES
    lanes = -(-slots // 128) * 128
    by_piece = jnp.transpose(t_amps.reshape(PIECES, chunk, columns // size, size), (0, 2, 1, 3))
    bf16, f32, i32 = jnp.bfloat16, jnp.float32, jnp.int32
    dma = pltpu.SemaphoreType.DMA
    out = pl.pallas_call(
        functools.partial(ladder_kernel, depth),
        out_shape=jax.ShapeDtypeStruct((half * 2, 2, rows, strip), f32),
        in_specs=[
            pl.BlockSpec(memory_space=pltpu.HBM),
            pl.BlockSpec(memory_space=pltpu.HBM),
            pl.BlockSpec(memory_space=pltpu.HBM),
            pl.BlockSpec(memory_space=pltpu.HBM),
        ],
        out_specs=pl.BlockSpec(memory_space=pl.ANY),
        scratch_shapes=[pltpu.VMEM((columns // size, chunk, size), bf16)] * (buffers * PIECES * 2) + [
            pltpu.VMEM((slots, size, size), bf16),
            pltpu.VMEM((slots, size, size), bf16),
            pltpu.VMEM(block_pos.shape, i32), pltpu.VMEM(block_count.shape, i32),
            pltpu.VMEM(block_pos.shape, i32), pltpu.VMEM(block_count.shape, i32),
            pltpu.VMEM((2, 8, lanes), i32),
            pltpu.SMEM((8, lanes), i32), pltpu.SMEM((8, lanes), i32),
            pltpu.VMEM((2, slots + 1, 4 * chunk, size), f32),
            pltpu.VMEM((depth, 2, 2, rows, strip), f32),
            pltpu.VMEM((half, 2, 2, rows, strip), f32),
            pltpu.VMEM((half, 2, rows, strip), f32),
            pltpu.VMEM((half, 2, rows, strip), f32),
            dma((PIECES,)),
            dma((5,)),
            dma((2, buffers, 2, PIECES)), dma((buffers, 2, PIECES)),
            dma((buffers, PIECES)), dma((buffers, PIECES)),
            dma((3,)), dma((3,)),
            dma((depth, 2, PIECES)), dma((depth, 2, PIECES)),
            dma((depth, PIECES)), dma((depth, PIECES)),
            dma((depth, PIECES)),
        ],
        compiler_params=pltpu.CompilerParams(
            collective_id=0, has_side_effects=True, vmem_limit_bytes=40 * 1024 * 1024
        ),
    )(*(pltpu.with_memory_space_constraint(a, pltpu.HBM) for a in (by_piece, v_blocks, block_pos)), block_count)
    return out.reshape(half * 4 * rows, strip)


def solution(mesh):
    in_specs = (
        P("wide", "narrow"),
        P("narrow", "wide", None, None, None),
        P("narrow", "wide", None),
        P("narrow", "wide"),
    )
    out_specs = P("narrow", "wide")
    wide_size, narrow_size = mesh.shape["wide"], mesh.shape["narrow"]

    def program(t_amps, v_blocks, block_pos, block_count):
        width = t_amps.shape[1]
        if narrow_size == 2 and wide_size >= 16 and wide_size % 8 == 0:
            body = functools.partial(ring_shards, width, wide_size)
        else:
            body = functools.partial(dense_shards, width)
        run = jax.shard_map(body, mesh=mesh, in_specs=in_specs, out_specs=out_specs, check_vma=False)
        return run(t_amps, v_blocks, block_pos, block_count)

    return program
```

time: 96.2 us -> 93.9 us (0.976)
  other arithmetic: 1.12 us -> 0 us
  Pallas kernels: 92.8 us -> 91.8 us
    pallas_call x1, Pallas kernels: 92.8 us -> 91.8 us  [ring_shards(): pl.pallas_call(functools.partial(ladder_kernel, depth), out_shape=jax.Sha...]
where the time goes in v3:
time: 93.9 us; the launch traced here: 93.8 us
  Pallas kernels  91.8 us (98%)
  local copies, waits for them, and re-layouts  1.32 us (1%)
    pallas_call x1, Pallas kernels, ring_shards(): pl.pallas_call(functools.partial(ladder_kernel, depth), out_shape=jax.Sha...  91.8 us

profile of v3, /device:TPU:1, one launch (start us, length us, event | category | flops | bytes accessed | tf_op | source)
XLA Modules:
  0.0 93.8 jit_solution(9764956001717204600)
XLA Ops:
  0.7 91.8 %shard_map.46 = f32[4,2,32,2048]{3,2,1,0:T(8,128)S(1)} custom-call(bf16[4,128,8,128]{3,2,1,0:T(8,128)(2,1)} %bitcast.5, bf16[1,1,64,128,128]{4,3,2,1,0:T(8,128)(2,1)} %v_tile.1, s32[1,1,64]{2,1,0:T(1,128)} %pos.1, s32[1,1]{1,0:T(1,128)S(6)} %copy.6.count), custom_call_target="tpu_custom_call" | custom-call | tf_op jit(solution)/shard_map/pallas_call | solution.py:335
  92.5 1.3 %copy.7 = f32[256,2048]{1,0:T(8,128)} copy(f32[256,2048]{1,0:T(8,128)S(1)} %bitcast.4) | data formatting | bytes 4194304

commit v4 on v3

--- a/solution.py
+++ b/solution.py
@@ -33,15 +33,16 @@
 def ladder_kernel(depth, t, v_tile, pos, count, out, *scratch):
     total = (2 * depth - 1) * PIECES * 2
     bufs = [[scratch[2 * (b * PIECES + q):2 * (b * PIECES + q) + 2] for q in range(PIECES)] for b in range(2 * depth - 1)]
-    (v_own, v_other, pos_own, count_own, pos_other, count_other, made, info_own, info_other, runs, part, core_in, y_out, own_out,
+    (v_own, v_other, pos_own, count_own, pos_other, count_other, made, info_own, info_other, runs, part, core_in, y_out, far_in,
      lay_sem, local_sem, z_send, z_recv, x_send, x_recv, one_send, one_recv, core_send, core_recv, y_send, y_recv,
-     own_sem) = scratch[total:]
+     far_send, far_recv) = scratch[total:]
     wide, core = lax.axis_index("wide"), lax.axis_index("narrow")
     z, y, x = wide // 4, (wide // 2) % 2, wide % 2
     up, down = (wide + 4, core), (wide - 4, core)
     across = (wide + 1 - 2 * x, core)
     beside = (wide + 2 - 4 * y, core)
     twin = (wide, 1 - core)
+    facing = (wide + 2 - 4 * y, 1 - core)
     half = depth // 2
     pieces, row_blocks, chunk, unused = t.shape
     v = v_tile.at[0, 0]
@@ -84,11 +85,12 @@
 
     def z_copy(b, kind, q, move):
         direction, device, unused, landing = move
-        return copy(z_ref(b, kind, q), z_ref(landing, kind, q), z_send.at[direction, b, kind, q], z_recv.at[landing, kind, q], device)
+        src = t.at[q] if (b, kind) == (0, 0) else z_ref(b, kind, q)
+        return copy(src, z_ref(landing, kind, q), z_send.at[direction, b, kind, q], z_recv.at[landing, kind, q], device)
 
     def x_copy(b, q, cols):
         mine_side, other_side = (ref.at[pl.ds(0, cols)] for ref in bufs[b][q])
-        return copy(mine_side, other_side, x_send.at[b, q], x_recv.at[b, q], across)
+        return copy(t.at[q] if b == 0 else mine_side, other_side, x_send.at[b, q], x_recv.at[b, q], across)
 
     def z_wait(b, kind, q):
         ref = z_ref(b, kind, q)
@@ -109,23 +111,18 @@
     def x_wait(k, b, way, q):
         crossing(k, way, lambda cols: x_copy(b, q, cols).wait_recv())
 
+    barrier = pltpu.get_barrier_semaphore()
+    for device in (across, beside, twin, facing):
+        pl.semaphore_signal(barrier, inc=1, device_id=device, device_id_type=MESH)
+    pl.when(has_up)(lambda: pl.semaphore_signal(barrier, inc=1, device_id=up, device_id_type=MESH))
+    pl.when(has_down)(lambda: pl.semaphore_signal(barrier, inc=1, device_id=down, device_id_type=MESH))
     lays = [pltpu.make_async_copy(t.at[q], bufs[0][q][0], lay_sem.at[q]) for q in range(pieces)]
     own_v = pltpu.make_async_copy(v, v_own, local_sem.at[0])
     own_p = pltpu.make_async_copy(pos, pos_own, local_sem.at[1])
     own_c = pltpu.make_async_copy(count, count_own, local_sem.at[2])
-    for lay in lays:
-        lay.start()
-    own_v.start()
-    own_p.start()
-    own_c.start()
-    barrier = pltpu.get_barrier_semaphore()
-    for device in (across, beside, twin):
-        pl.semaphore_signal(barrier, inc=1, device_id=device, device_id_type=MESH)
-    pl.when(has_up)(lambda: pl.semaphore_signal(barrier, inc=1, device_id=up, device_id_type=MESH))
-    pl.when(has_down)(lambda: pl.semaphore_signal(barrier, inc=1, device_id=down, device_id_type=MESH))
-    for lay in lays:
-        lay.wait()
-    pl.semaphore_wait(barrier, 3 + has_up.astype(jnp.int32) + has_down.astype(jnp.int32))
+    for each in (*lays, own_v, own_p, own_c):
+        each.start()
+    pl.semaphore_wait(barrier, 4 + has_up.astype(jnp.int32) + has_down.astype(jnp.int32))
 
     vy = copy(v, v_other, one_send.at[0], one_recv.at[0], beside)
     py = copy(pos, pos_other, one_send.at[1], one_recv.at[1], beside)
@@ -164,6 +161,11 @@
             return [(x, (0,), tuple(range(pieces)))] + tail
         return [(pl.ds(0, 2), (0, 1), (q, q + 1)) for q in range(0, pieces, 2)]
 
+    final = len(steps(depth - 1)) - 1
+
+    def is_last(k, n):
+        return (k, n) == (depth - 1, final)
+
     def span(k, n):
         sides, unused, qs = steps(k)[n]
         return sides, pl.ds(qs[0] * chunk, len(qs) * chunk)
@@ -178,8 +180,8 @@
     def y_copy(zp, k, n):
         return copy(y_out.at[zp % half, *span(k, n)], target(zp, k, n), y_send.at[zp, n], y_recv.at[zp, n], beside)
 
-    def own_copy(zp, k, n):
-        return pltpu.make_async_copy(own_out.at[zp % half, *span(k, n)], target(zp, k, n), own_sem.at[zp, n])
+    def far_copy(zp, slot, device):
+        return copy(part.at[zp, 0, *span(depth - 1, final)], far_in.at[slot], far_send.at[slot], far_recv.at[slot], device)
 
     def mine(zp):
         return zp // half == core
@@ -221,7 +223,11 @@
                 for i, side in enumerate(sides):
                     part[zp, strip, x if side == 0 else 1 - x, span(k, n)[1], c * size:(c + 1) * size] = (
                         value[i * len(qs) * chunk:(i + 1) * len(qs) * chunk])
-            pl.when(jnp.logical_not(mine(zp)))(lambda: core_copy(zp, strip, k, n).start())
+            if is_last(k, n) and strip == 0:
+                pl.when(mine(zp))(lambda: far_copy(zp, 0, beside).start())
+                pl.when(jnp.logical_not(mine(zp)))(lambda: far_copy(zp, 1, facing).start())
+            else:
+                pl.when(jnp.logical_not(mine(zp)))(lambda: core_copy(zp, strip, k, n).start())
 
     def compute(k, n, ahead=None):
         for b, zp, valid, way in shards(k):
@@ -243,12 +249,16 @@
     def finish(k, n, only=None):
         for b, zp, valid, way in shards(k):
             def run(zp=zp):
-                core_copy(zp, 0, k, n).wait_recv()
-                y_out[zp % half, *span(k, n)] = part[zp, 0, *span(k, n)] + core_in[zp % half, 0, *span(k, n)]
-                y_copy(zp, k, n).start()
+                if not is_last(k, n):
+                    core_copy(zp, 0, k, n).wait_recv()
+                    y_out[zp % half, *span(k, n)] = part[zp, 0, *span(k, n)] + core_in[zp % half, 0, *span(k, n)]
+                    y_copy(zp, k, n).start()
                 core_copy(zp, 1, k, n).wait_recv()
-                own_out[zp % half, *span(k, n)] = part[zp, 1, *span(k, n)] + core_in[zp % half, 1, *span(k, n)]
-                own_copy(zp, k, n).start()
+                out[zp % half * 2 + y, *span(k, n)] = part[zp, 1, *span(k, n)] + core_in[zp % half, 1, *span(k, n)]
+                if is_last(k, n):
+                    for slot in (0, 1):
+                        far_copy(zp, slot, beside).wait_recv()
+                    out[zp % half * 2 + 1 - y, *span(k, n)] = far_in[0] + far_in[1]
 
             if only is None:
                 guarded(both(valid, mine(zp)), run)
@@ -275,7 +285,8 @@
         each.start()
     for each in into:
         each.wait()
-    own_v.wait()
+    for each in (*lays, own_v):
+        each.wait()
     vy.wait_recv()
     compute(0, 0)
     compute(0, 1)
@@ -297,7 +308,6 @@
                 finish(k, n)
     compute(depth - 1, 0)
     finish(depth - 2, 1)
-    final = len(steps(depth - 1)) - 1
     for n in range(1, final):
         compute(depth - 1, n)
         finish(depth - 1, n - 1)
@@ -315,8 +325,12 @@
                     guarded(both(is_end(k, way), move[2]), lambda move=move: [z_copy(b, 1, q, move).wait_send() for q in range(pieces)] and None)
                 crossing(k, way, lambda cols: [x_copy(b, q, cols).wait_send() for q in range(pieces)] and None)
                 other = jnp.logical_not(mine(zp))
-                pl.when(other)(lambda: [core_copy(zp, j, k, n).wait_send() for j in (0, 1) for n in range(len(steps(k)))] and None)
-                pl.when(mine(zp))(lambda: [(y_copy(zp, k, n).wait(), own_copy(zp, k, n).wait()) for n in range(len(steps(k)))] and None)
+                pl.when(other)(lambda: [core_copy(zp, j, k, n).wait_send() for j in (0, 1) for n in range(len(steps(k)))
+                                        if j == 1 or not is_last(k, n)] and None)
+                if k == depth - 1:
+                    pl.when(other)(lambda: far_copy(zp, 1, facing).wait_send())
+                    pl.when(mine(zp))(lambda: far_copy(zp, 0, beside).wait_send())
+                pl.when(mine(zp))(lambda: [y_copy(zp, k, n).wait() for n in range(len(steps(k))) if not is_last(k, n)] and None)
 
             guarded(valid, run)
 
@@ -341,7 +355,7 @@
             pl.BlockSpec(memory_space=pltpu.HBM),
             pl.BlockSpec(memory_space=pltpu.HBM),
         ],
-        out_specs=pl.BlockSpec(memory_space=pl.ANY),
+        out_specs=pl.BlockSpec(memory_space=pltpu.VMEM),
         scratch_shapes=[pltpu.VMEM((columns // size, chunk, size), bf16)] * (buffers * PIECES * 2) + [
             pltpu.VMEM((slots, size, size), bf16),
             pltpu.VMEM((slots, size, size), bf16),
@@ -353,7 +367,7 @@
             pltpu.VMEM((depth, 2, 2, rows, strip), f32),
             pltpu.VMEM((half, 2, 2, rows, strip), f32),
             pltpu.VMEM((half, 2, rows, strip), f32),
-            pltpu.VMEM((half, 2, rows, strip), f32),
+            pltpu.VMEM((2, chunk, strip), f32),
             dma((PIECES,)),
             dma((5,)),
             dma((2, buffers, 2, PIECES)), dma((buffers, 2, PIECES)),
@@ -361,7 +375,7 @@
             dma((3,)), dma((3,)),
             dma((depth, 2, PIECES)), dma((depth, 2, PIECES)),
             dma((depth, PIECES)), dma((depth, PIECES)),
-            dma((depth, PIECES)),
+            dma((2,)), dma((2,)),
         ],
         compiler_params=pltpu.CompilerParams(
             collective_id=0, has_side_effects=True, vmem_limit_bytes=40 * 1024 * 1024

time: 93.9 us -> 93.7 us (level)
  no operation moved by 1% of the time
where the time goes in v4:
time: 93.7 us; the launch traced here: 93.5 us
  Pallas kernels  91.6 us (98%)
  local copies, waits for them, and re-layouts  1.32 us (1%)
    pallas_call x1, Pallas kernels, ring_shards(): pl.pallas_call(functools.partial(ladder_kernel, depth), out_shape=jax.Sha...  91.6 us

profile of v4, /device:TPU:1, one launch (start us, length us, event | category | flops | bytes accessed | tf_op | source)
XLA Modules:
  0.0 93.5 jit_solution(3685084813105787154)
XLA Ops:
  0.7 91.6 %shard_map.46 = f32[4,2,32,2048]{3,2,1,0:T(8,128)S(1)} custom-call(bf16[4,128,8,128]{3,2,1,0:T(8,128)(2,1)} %bitcast.5, bf16[1,1,64,128,128]{4,3,2,1,0:T(8,128)(2,1)} %v_tile.1, s32[1,1,64]{2,1,0:T(1,128)} %pos.1, s32[1,1]{1,0:T(1,128)S(6)} %copy.6.count), custom_call_target="tpu_custom_call" | custom-call | tf_op jit(solution)/shard_map/pallas_call | solution.py:349
  92.2 1.3 %copy.7 = f32[256,2048]{1,0:T(8,128)} copy(f32[256,2048]{1,0:T(8,128)S(1)} %bitcast.4) | data formatting | bytes 4194304

commit v5 on v4

--- a/solution.py
+++ b/solution.py
@@ -85,12 +85,12 @@
 
     def z_copy(b, kind, q, move):
         direction, device, unused, landing = move
-        src = t.at[q] if (b, kind) == (0, 0) else z_ref(b, kind, q)
+        src = z_ref(b, kind, q)
         return copy(src, z_ref(landing, kind, q), z_send.at[direction, b, kind, q], z_recv.at[landing, kind, q], device)
 
     def x_copy(b, q, cols):
         mine_side, other_side = (ref.at[pl.ds(0, cols)] for ref in bufs[b][q])
-        return copy(t.at[q] if b == 0 else mine_side, other_side, x_send.at[b, q], x_recv.at[b, q], across)
+        return copy(mine_side, other_side, x_send.at[b, q], x_recv.at[b, q], across)
 
     def z_wait(b, kind, q):
         ref = z_ref(b, kind, q)
@@ -120,8 +120,10 @@
     own_v = pltpu.make_async_copy(v, v_own, local_sem.at[0])
     own_p = pltpu.make_async_copy(pos, pos_own, local_sem.at[1])
     own_c = pltpu.make_async_copy(count, count_own, local_sem.at[2])
-    for each in (*lays, own_v, own_p, own_c):
+    for each in (*lays, own_p, own_c):
         each.start()
+    for lay in lays:
+        lay.wait()
     pl.semaphore_wait(barrier, 4 + has_up.astype(jnp.int32) + has_down.astype(jnp.int32))
 
     vy = copy(v, v_other, one_send.at[0], one_recv.at[0], beside)
@@ -134,6 +136,7 @@
     py.start()
     cy.start()
     vy.start()
+    own_v.start()
 
     def relay(k, kind, q):
         for b, zp, valid, way in shards(k):
@@ -229,16 +232,18 @@
             else:
                 pl.when(jnp.logical_not(mine(zp)))(lambda: core_copy(zp, strip, k, n).start())
 
-    def compute(k, n, ahead=None):
+    def compute(k, n, ahead=None, strips=(0, 1), landed=False):
         for b, zp, valid, way in shards(k):
             def run(b=b, zp=zp, way=way):
                 for q in steps(k)[n][2]:
+                    if landed:
+                        continue
                     if 0 < k < depth - 1 or n > 0 and k > 0:
                         x_wait(k, b, way, q)
                     if n > 0 and k == depth - 1:
                         z_wait(b, 1, q)
                 if ahead is None:
-                    products(b, zp, k, n, (0, 1), 16)
+                    products(b, zp, k, n, strips, 16)
                 else:
                     products(b, zp, k, n, (0,), 32)
                     finish(k, ahead, b)
@@ -246,15 +251,16 @@
 
             guarded(valid, run)
 
-    def finish(k, n, only=None):
+    def finish(k, n, only=None, strips=(0, 1)):
         for b, zp, valid, way in shards(k):
             def run(zp=zp):
-                if not is_last(k, n):
+                if 0 in strips and not is_last(k, n):
                     core_copy(zp, 0, k, n).wait_recv()
                     y_out[zp % half, *span(k, n)] = part[zp, 0, *span(k, n)] + core_in[zp % half, 0, *span(k, n)]
                     y_copy(zp, k, n).start()
-                core_copy(zp, 1, k, n).wait_recv()
-                out[zp % half * 2 + y, *span(k, n)] = part[zp, 1, *span(k, n)] + core_in[zp % half, 1, *span(k, n)]
+                if 1 in strips:
+                    core_copy(zp, 1, k, n).wait_recv()
+                    out[zp % half * 2 + y, *span(k, n)] = part[zp, 1, *span(k, n)] + core_in[zp % half, 1, *span(k, n)]
                 if is_last(k, n):
                     for slot in (0, 1):
                         far_copy(zp, slot, beside).wait_recv()
@@ -270,34 +276,38 @@
     for q in range(pieces):
         relay(1, 0, q)
         relay_own(q)
+    into = [pltpu.make_async_copy(made.at[strip], tables[strip][1], local_sem.at[3 + strip]) for strip in (0, 1)]
     own_p.wait()
     own_c.wait()
     chain(pos_own, count_own, 1)
+    into[1].start()
     py.wait_recv()
     cy.wait_recv()
     chain(pos_other, count_other, 0)
+    into[0].start()
+    for each in (*into, own_v):
+        each.wait()
+    for n in range(len(steps(0))):
+        compute(0, n, strips=(1,))
     for k in range(2, depth - 1):
         for q in range(pieces):
             relay(k - 1, 1, q)
             relay(k, 0, q)
-    into = [pltpu.make_async_copy(made.at[strip], tables[strip][1], local_sem.at[3 + strip]) for strip in (0, 1)]
-    for each in into:
-        each.start()
-    for each in into:
-        each.wait()
-    for each in (*lays, own_v):
-        each.wait()
     vy.wait_recv()
-    compute(0, 0)
-    compute(0, 1)
+    compute(0, 0, strips=(0,), landed=True)
+    compute(0, 1, strips=(0,), landed=True)
     finish(0, 0)
-    compute(1, 0)
+    compute(1, 0, strips=(0,))
     finish(0, 1)
+    compute(1, 1, strips=(0,))
+    finish(1, 0, strips=(0,))
     for q in range(pieces):
         relay(depth - 2, 1, q)
-    compute(1, 1)
-    finish(1, 0)
-    finish(1, 1)
+    finish(1, 1, strips=(0,))
+    for n in range(len(steps(1))):
+        compute(1, n, strips=(1,), landed=True)
+    for n in range(len(steps(1))):
+        finish(1, n, strips=(1,))
     for k in range(2, depth - 1):
         for n in range(len(steps(k))):
             if k == depth - 2:
@@ -308,9 +318,11 @@
                 finish(k, n)
     compute(depth - 1, 0)
     finish(depth - 2, 1)
+    finish(depth - 1, 0)
     for n in range(1, final):
         compute(depth - 1, n)
-        finish(depth - 1, n - 1)
+        if n > 1:
+            finish(depth - 1, n - 1)
     compute(depth - 1, final, final - 1)
     finish(depth - 1, final)
 

time: 93.7 us -> 93.4 us (level)
  no operation moved by 1% of the time
where the time goes in v5:
time: 93.4 us; the launch traced here: 93.3 us
  Pallas kernels  91.3 us (98%)
  local copies, waits for them, and re-layouts  1.32 us (1%)
    pallas_call x1, Pallas kernels, ring_shards(): pl.pallas_call(functools.partial(ladder_kernel, depth), out_shape=jax.Sha...  91.3 us

profile of v5, /device:TPU:1, one launch (start us, length us, event | category | flops | bytes accessed | tf_op | source)
XLA Modules:
  0.0 93.3 jit_solution(8653071538672165455)
XLA Ops:
  0.7 91.3 %shard_map.46 = f32[4,2,32,2048]{3,2,1,0:T(8,128)S(1)} custom-call(bf16[4,128,8,128]{3,2,1,0:T(8,128)(2,1)} %bitcast.5, bf16[1,1,64,128,128]{4,3,2,1,0:T(8,128)(2,1)} %v_tile.1, s32[1,1,64]{2,1,0:T(1,128)} %pos.1, s32[1,1]{1,0:T(1,128)S(6)} %copy.6.count), custom_call_target="tpu_custom_call" | custom-call | tf_op jit(solution)/shard_map/pallas_call | solution.py:361
  92.0 1.3 %copy.7 = f32[256,2048]{1,0:T(8,128)} copy(f32[256,2048]{1,0:T(8,128)S(1)} %bitcast.4) | data formatting | bytes 4194304

commit v6 on v5

--- a/solution.py
+++ b/solution.py
@@ -122,14 +122,13 @@
     own_c = pltpu.make_async_copy(count, count_own, local_sem.at[2])
     for each in (*lays, own_p, own_c):
         each.start()
-    for lay in lays:
-        lay.wait()
     pl.semaphore_wait(barrier, 4 + has_up.astype(jnp.int32) + has_down.astype(jnp.int32))
 
     vy = copy(v, v_other, one_send.at[0], one_recv.at[0], beside)
     py = copy(pos, pos_other, one_send.at[1], one_recv.at[1], beside)
     cy = copy(count, count_other, one_send.at[2], one_recv.at[2], beside)
     for q in range(pieces):
+        lays[q].wait()
         for move in onward(0, None):
             guarded(move[2], lambda move=move: z_copy(0, 0, q, move).start())
         x_start(0, 0, None, q)

time: 93.4 us -> 93.4 us (level)
  no operation moved by 1% of the time
where the time goes in v6:
time: 93.4 us; the launch traced here: 93.3 us
  Pallas kernels  91.3 us (98%)
  local copies, waits for them, and re-layouts  1.32 us (1%)
    pallas_call x1, Pallas kernels, ring_shards(): pl.pallas_call(functools.partial(ladder_kernel, depth), out_shape=jax.Sha...  91.3 us

profile of v6, /device:TPU:1, one launch (start us, length us, event | category | flops | bytes accessed | tf_op | source)
XLA Modules:
  0.0 93.3 jit_solution(16837719042191226461)
XLA Ops:
  0.7 91.3 %shard_map.46 = f32[4,2,32,2048]{3,2,1,0:T(8,128)S(1)} custom-call(bf16[4,128,8,128]{3,2,1,0:T(8,128)(2,1)} %bitcast.5, bf16[1,1,64,128,128]{4,3,2,1,0:T(8,128)(2,1)} %v_tile.1, s32[1,1,64]{2,1,0:T(1,128)} %pos.1, s32[1,1]{1,0:T(1,128)S(6)} %copy.6.count), custom_call_target="tpu_custom_call" | custom-call | tf_op jit(solution)/shard_map/pallas_call | solution.py:360
  92.0 1.3 %copy.7 = f32[256,2048]{1,0:T(8,128)} copy(f32[256,2048]{1,0:T(8,128)S(1)} %bitcast.4) | data formatting | bytes 4194304

commit v7 on v6

--- a/solution.py
+++ b/solution.py
@@ -279,19 +279,20 @@
     own_p.wait()
     own_c.wait()
     chain(pos_own, count_own, 1)
-    into[1].start()
     py.wait_recv()
     cy.wait_recv()
     chain(pos_other, count_other, 0)
-    into[0].start()
-    for each in (*into, own_v):
+    into[1].start()
+    for each in (into[1], own_v):
         each.wait()
     for n in range(len(steps(0))):
         compute(0, n, strips=(1,))
+    into[0].start()
     for k in range(2, depth - 1):
         for q in range(pieces):
             relay(k - 1, 1, q)
             relay(k, 0, q)
+    into[0].wait()
     vy.wait_recv()
     compute(0, 0, strips=(0,), landed=True)
     compute(0, 1, strips=(0,), landed=True)

time: 93.4 us -> 93.4 us (level)
  no operation moved by 1% of the time
where the time goes in v7:
time: 93.4 us; the launch traced here: 93.3 us
  Pallas kernels  91.3 us (98%)
  local copies, waits for them, and re-layouts  1.32 us (1%)
    pallas_call x1, Pallas kernels, ring_shards(): pl.pallas_call(functools.partial(ladder_kernel, depth), out_shape=jax.Sha...  91.3 us

profile of v7, /device:TPU:1, one launch (start us, length us, event | category | flops | bytes accessed | tf_op | source)
XLA Modules:
  0.0 93.3 jit_solution(7401195869488801479)
XLA Ops:
  0.7 91.3 %shard_map.46 = f32[4,2,32,2048]{3,2,1,0:T(8,128)S(1)} custom-call(bf16[4,128,8,128]{3,2,1,0:T(8,128)(2,1)} %bitcast.5, bf16[1,1,64,128,128]{4,3,2,1,0:T(8,128)(2,1)} %v_tile.1, s32[1,1,64]{2,1,0:T(1,128)} %pos.1, s32[1,1]{1,0:T(1,128)S(6)} %copy.6.count), custom_call_target="tpu_custom_call" | custom-call | tf_op jit(solution)/shard_map/pallas_call | solution.py:361
  92.0 1.3 %copy.7 = f32[256,2048]{1,0:T(8,128)} copy(f32[256,2048]{1,0:T(8,128)S(1)} %bitcast.4) | data formatting | bytes 4194304
